TPU v7x, 32 devices: a whole 2x2x4 slice. The times are simulated.
32 devices in a mesh: ep: 8 (over z, y), tp: 4 (over x, core).
Axes of the slice: x: 2, y: 2, z: 4, core: 2. Of those that a mesh axis runs over, the one named last changes fastest.
Arguments:
- tokens: bfloat16 [1024, 4096], P('ep', 'tp'), may hold values from -6 to 6
- out_grad: bfloat16 [1024, 4096], P('ep', 'tp'), may hold values from -6 to 6
- expert_ids: int32 [1024, 4], P('ep'), may hold values from 0 to 7, all different within a row; in each aligned block of 128 rows (0 to 127, 128 to 255, ...) at most 72 rows name the same one
- route_probs: float32 [1024, 4], P('ep'), may hold values from 0.05 to 0.5
- w_gate: bfloat16 [8, 4096, 768], P('ep', 'tp'), may hold values from -0.09375 to 0.09375
- w_up: bfloat16 [8, 4096, 768], P('ep', 'tp'), may hold values from -0.09375 to 0.09375
- w_down: bfloat16 [8, 768, 4096], P('ep', None, 'tp'), may hold values from -0.21875 to 0.21875
Outputs:
- grad_tokens: bfloat16 [1024, 4096], P('ep', 'tp')
- fisher_gate: bfloat16 [8, 4096, 768], P('ep', 'tp')
- fisher_up: bfloat16 [8, 4096, 768], P('ep', 'tp')
- fisher_down: bfloat16 [8, 768, 4096], P('ep', None, 'tp')
Inputs may be any that keep to these rules, and one draw needn't show every extreme that they name: `expert_ids`: each token names 4 different experts; among the tokens of one index of ep no expert is named by more than 72 tokens, a bound that some block reaches.
All inputs are finite; a program needn't handle non-finite values.
Results may differ from a plain program's by a relative error of at most 0.03.
Values may be sent and summed in bfloat16 or wider, within the bound.
A program may use at most 128 MiB of HBM per device.

v0:
```python
import jax
import jax.numpy as jnp
from jax import lax
from jax.sharding import PartitionSpec as P


def contract_rows(left, right):
    return lax.dot_general(
        left, right, (((0,), (0,)), ((), ())), preferred_element_type=jnp.float32
    )


def contract_cols(left, right):
    return lax.dot_general(
        left, right, (((1,), (1,)), ((), ())), preferred_element_type=jnp.float32
    )


def swiglu_back(gate, up, dact):
    sig = jax.nn.sigmoid(gate)
    act = (gate * sig * up).astype(jnp.bfloat16)
    dgate = (dact * up * sig * (1.0 + gate * (1.0 - sig))).astype(jnp.bfloat16)
    dup = (dact * gate * sig).astype(jnp.bfloat16)
    return (act, dgate, dup)


def squared(values):
    return jnp.square(values.astype(jnp.float32)).astype(jnp.bfloat16)


def on_device(tokens, out_grad, expert_ids, route_probs, w_gate, w_up, w_down):
    tok_rows = tokens.shape[0]
    width_part = tokens.shape[1]
    top_count = expert_ids.shape[1]
    experts = lax.axis_size("ep")
    capacity = tok_rows * top_count * 9 // (8 * experts)
    assigns = tok_rows * top_count
    flat_ids = expert_ids.reshape(-1)
    onehot = (flat_ids[:, None] == jnp.arange(experts, dtype=jnp.int32)[None, :]).astype(jnp.int32)
    ranks = jnp.sum((jnp.cumsum(onehot, 0) - onehot) * onehot, 1)
    slot_index = flat_ids * capacity + ranks
    table = (
        jnp.full((experts * capacity,), assigns, jnp.int32)
        .at[slot_index]
        .set(jnp.arange(assigns, dtype=jnp.int32))
    )
    token_of = table // top_count
    padded_x = jnp.concatenate([tokens, jnp.zeros((1, width_part), tokens.dtype)], 0)
    padded_dy = jnp.concatenate([out_grad, jnp.zeros((1, width_part), out_grad.dtype)], 0)
    padded_p = jnp.concatenate([route_probs.reshape(-1), jnp.zeros((1,), jnp.float32)], 0)
    send_x = padded_x[token_of].reshape(experts, capacity, width_part)
    send_dy = (padded_dy[token_of].astype(jnp.float32) * padded_p[table][:, None]).astype(
        jnp.bfloat16
    )
    send_dy = send_dy.reshape(experts, capacity, width_part)
    gate_mat = w_gate[0]
    up_mat = w_up[0]
    down_mat = w_down[0]
    recv_x, recv_dy = (
        lax.all_to_all(send_x, "ep", split_axis=0, concat_axis=0, tiled=True),
        lax.all_to_all(send_dy, "ep", split_axis=0, concat_axis=0, tiled=True),
    )
    recv_x = recv_x.reshape(-1, width_part)
    recv_dy = recv_dy.reshape(-1, width_part)
    gate_part = jnp.dot(recv_x, gate_mat, preferred_element_type=jnp.float32)
    up_part = jnp.dot(recv_x, up_mat, preferred_element_type=jnp.float32)
    dact_part = contract_cols(recv_dy, down_mat)
    gate, up, dact = (
        lax.psum(gate_part.astype(jnp.bfloat16), "tp").astype(jnp.float32),
        lax.psum(up_part.astype(jnp.bfloat16), "tp").astype(jnp.float32),
        lax.psum(dact_part.astype(jnp.bfloat16), "tp").astype(jnp.float32),
    )
    act, dgate, dup = swiglu_back(gate, up, dact)
    dx_rows = (contract_cols(dgate, gate_mat) + contract_cols(dup, up_mat)).astype(jnp.bfloat16)
    returned = lax.all_to_all(
        dx_rows.reshape(experts, capacity, width_part),
        "ep",
        split_axis=0,
        concat_axis=0,
        tiled=True,
    )
    scale = 1.0 / tok_rows
    x_sq = squared(recv_x)
    fisher_gate = (contract_rows(x_sq, squared(dgate)) * scale).astype(jnp.bfloat16)[None]
    fisher_up = (contract_rows(x_sq, squared(dup)) * scale).astype(jnp.bfloat16)[None]
    fisher_down = (contract_rows(squared(act), squared(recv_dy)) * scale).astype(jnp.bfloat16)[None]
    pulled = returned.reshape(experts * capacity, width_part)[slot_index].astype(jnp.float32)
    grad_tokens = jnp.sum(pulled.reshape(tok_rows, top_count, width_part), 1).astype(jnp.bfloat16)
    return (grad_tokens, fisher_gate, fisher_up, fisher_down)


def solution(mesh):
    in_specs = (
        P("ep", "tp"),
        P("ep", "tp"),
        P("ep", None),
        P("ep", None),
        P("ep", "tp", None),
        P("ep", "tp", None),
        P("ep", None, "tp"),
    )
    out_specs = (P("ep", "tp"), P("ep", "tp", None), P("ep", "tp", None), P("ep", None, "tp"))
    return jax.shard_map(
        on_device, mesh=mesh, in_specs=in_specs, out_specs=out_specs, check_vma=False
    )
```

profile of v0, /device:TPU:0, one launch (start us, length us, event | category | flops | bytes accessed | tf_op | source)
XLA Modules:
  0.0 202.3 jit_solution(541118483908250791)
XLA Ops:
  9.2 1.1 reduce-window.6
  10.7 2.4 %scatter_custom_fusion = s32[576]{0:T(1024)S(1)} fusion(s32[512]{0:T(512)S(1)} %bitcast.50, s32[512]{0:T(512)S(1)} %iota.11, s32[]{:T(128)} %constant.15.clone.1), kind=kCustom, calls=%fused_computation.68 | custom fusion | bytes 2308 | tf_op jit(solution)/shard_map/scatter | solution.py:45
  14.2 3.4 %gather_fusion.2 = bf16[576,1024]{1,0:T(8,128)(2,1)} fusion(bf16[129,1024]{1,0:T(8,128)(2,1)S(1)} %concatenate.11, s32[1024]{0:T(1024)S(1)} %get-tuple-element.10), kind=kCustom, calls=%fused_computation.2 | custom fusion | bytes 2361600 | tf_op jit(solution)/shard_map/gather | solution.py:51
  17.6 7.4 %all-to-all-start.1 = ((bf16[8,72,1024]{2,1,0:T(8,128)(2,1)}), bf16[8,72,1024]{2,1,0:T(8,128)(2,1)}, u32[]{:S(2)}, u32[]{:S(2)}) async-start(bf16[8,72,1024]{2,1,0:T(8,128)(2,1)} %bitcast.7), calls=%async_computation.1 | async-start | bytes 2359296 | tf_op jit(solution)/shard_map/all_to_all | solution.py:60
  25.1 2.9 %gather_fusion = bf16[576,1024]{1,0:T(8,128)(2,1)S(1)} fusion(bf16[129,1024]{1,0:T(8,128)(2,1)S(1)} %concatenate.9, s32[1024]{0:T(1024)S(1)} %get-tuple-element.10), kind=kCustom, calls=%fused_computation | custom fusion | bytes 2361600 | tf_op jit(solution)/shard_map/gather | solution.py:52
  28.2 2.6 %gather_fusion.1 = f32[576]{0:T(1024)S(1)} fusion(f32[513]{0:T(1024)S(1)} %pad_maximum_fusion, s32[1024]{0:T(1024)S(1)} %get-tuple-element.9), kind=kCustom, calls=%fused_computation.1 | custom fusion | bytes 6912 | tf_op jit(solution)/shard_map/gather | solution.py:52
  30.9 1.3 fusion
  32.2 21.6 %all-to-all-done.1 = bf16[8,72,1024]{2,1,0:T(8,128)(2,1)} async-done(((bf16[8,72,1024]{2,1,0:T(8,128)(2,1)}), bf16[8,72,1024]{2,1,0:T(8,128)(2,1)}, u32[]{:S(2)}, u32[]{:S(2)}) %all-to-all-start.1) | async-done | bytes 1179680 | tf_op jit(solution)/shard_map/all_to_all | solution.py:60
  53.8 3.6 %all-to-all-start = ((bf16[8,72,1024]{2,1,0:T(8,128)(2,1)}), bf16[8,72,1024]{2,1,0:T(8,128)(2,1)S(1)}, u32[]{:S(2)}, u32[]{:S(2)}) async-start(bf16[8,72,1024]{2,1,0:T(8,128)(2,1)} %fusion), calls=%async_computation | async-start | bytes 2359296 | tf_op jit(solution)/shard_map/all_to_all | solution.py:61
  57.4 3.8 %fusion.26 = bf16[576,768]{1,0:T(8,128)(2,1)} fusion(bf16[576,1024]{1,0:T(8,128)(2,1)} %bitcast.8, bf16[1,1024,768]{2,1,0:T(8,128)(2,1)} %param.12), kind=kOutput, calls=%fused_computation.45 | convolution fusion | flops 906412032 | bytes 3637248 | tf_op jit(solution)/shard_map/dot_general | solution.py:66
  61.2 3.3 %fusion.29 = bf16[576,768]{1,0:T(8,128)(2,1)} fusion(bf16[576,1024]{1,0:T(8,128)(2,1)} %bitcast.8, bf16[1,1024,768]{2,1,0:T(8,128)(2,1)S(1)} %copy-done), kind=kOutput, calls=%fused_computation.46 | convolution fusion | flops 906412032 | bytes 3637248 | tf_op jit(solution)/shard_map/dot_general | solution.py:65
  64.5 21.6 %all-to-all-done = bf16[8,72,1024]{2,1,0:T(8,128)(2,1)S(1)} async-done(((bf16[8,72,1024]{2,1,0:T(8,128)(2,1)}), bf16[8,72,1024]{2,1,0:T(8,128)(2,1)S(1)}, u32[]{:S(2)}, u32[]{:S(2)}) %all-to-all-start) | async-done | bytes 1179680 | tf_op jit(solution)/shard_map/all_to_all | solution.py:61
  86.1 3.9 %fusion.23 = bf16[576,768]{1,0:T(8,128)(2,1)} fusion(bf16[576,1024]{1,0:T(8,128)(2,1)S(1)} %bitcast.47, bf16[1,768,1024]{2,1,0:T(8,128)(2,1)} %param.13), kind=kOutput, calls=%fused_computation.44 | convolution fusion | flops 906412032 | bytes 3637248 | tf_op jit(solution)/shard_map/dot_general | solution.py:14
  90.0 59.7 %all-reduce.5.cloned.1.call-done = (bf16[576,768]{1,0:T(8,128)(2,1)}, bf16[576,768]{1,0:T(8,128)(2,1)}, bf16[576,768]{1,0:T(8,128)(2,1)}) async-done(((bf16[576,768]{1,0:T(8,128)(2,1)}, bf16[576,768]{1,0:T(8,128)(2,1)}, bf16[576,768]{1,0:T(8,128)(2,1)}), (bf16[576,768]{1,0:T(8,128)(2,1)}, bf16[576,768]{1,0:T(8,128)(2,1)}, bf16[576,768]{1,0:T(8,128)(2,1)})) %all-reduce.5.cloned.1.call-update) | async-done | bytes 2654224 | tf_op jit(solution)/shard_map/psum | solution.py:70
  149.7 3.3 %fusion.11 = f32[576,1024]{1,0:T(8,128)S(1)} fusion(bf16[1,1024,768]{2,1,0:T(8,128)(2,1)S(1)} %copy-done, bf16[576,768]{1,0:T(8,128)(2,1)} %get-tuple-element.4, bf16[576,768]{1,0:T(8,128)(2,1)} %get-tuple-element.5, bf16[576,768]{1,0:T(8,128)(2,1)} %get-tuple-element.6), kind=kOutput, calls=%fused_computation.32 | convolution fusion | flops 911720448 | bytes 6586368 | tf_op jit(solution)/shard_map/dot_general | solution.py:14
  153.1 2.2 %add_convert_fusion = bf16[576,1024]{1,0:T(8,128)(2,1)} fusion(f32[576,1024]{1,0:T(8,128)S(1)} %fusion.11, bf16[1,1024,768]{2,1,0:T(8,128)(2,1)S(1)} %copy-done.4, bf16[576,768]{1,0:T(8,128)(2,1)S(1)} %copy-done.8, bf16[576,768]{1,0:T(8,128)(2,1)S(1)} %copy-done.6), kind=kOutput, calls=%fused_computation.16 | convolution fusion | flops 910688256 | bytes 6881280 | tf_op jit(solution)/shard_map/dot_general | solution.py:14
  155.3 5.5 %all-to-all-start.2 = ((bf16[8,72,1024]{2,1,0:T(8,128)(2,1)}), bf16[8,72,1024]{2,1,0:T(8,128)(2,1)S(1)}, u32[]{:S(2)}, u32[]{:S(2)}) async-start(bf16[8,72,1024]{2,1,0:T(8,128)(2,1)} %bitcast.49), calls=%async_computation.2 | async-start | bytes 2359296 | tf_op jit(solution)/shard_map/all_to_all | solution.py:75
  160.9 4.8 %fusion.22 = bf16[1,768,1024]{2,1,0:T(8,128)(2,1)} fusion(bf16[576,1024]{1,0:T(8,128)(2,1)} %bitcast.48, bf16[576,768]{1,0:T(8,128)(2,1)} %get-tuple-element.4, bf16[576,768]{1,0:T(8,128)(2,1)} %get-tuple-element.6), kind=kOutput, calls=%fused_computation.43 | convolution fusion | flops 914178048 | bytes 4521984 | tf_op jit(solution)/shard_map/dot_general | solution.py:8
  165.7 4.2 %fusion.21 = bf16[1,1024,768]{2,1,0:T(8,128)(2,1)} fusion(bf16[576,1024]{1,0:T(8,128)(2,1)} %bitcast.8, bf16[576,768]{1,0:T(8,128)(2,1)S(1)} %copy-done.9, bf16[576,768]{1,0:T(8,128)(2,1)S(1)} %copy-done.7), kind=kOutput, calls=%fused_computation.42 | convolution fusion | flops 914178048 | bytes 4521984 | tf_op jit(solution)/shard_map/dot_general | solution.py:8
  169.9 4.4 %fusion.20 = bf16[1,1024,768]{2,1,0:T(8,128)(2,1)} fusion(bf16[576,1024]{1,0:T(8,128)(2,1)} %bitcast.8, bf16[576,768]{1,0:T(8,128)(2,1)S(1)} %copy-done.5, bf16[576,768]{1,0:T(8,128)(2,1)S(1)} %copy-done.7, bf16[576,768]{1,0:T(8,128)(2,1)S(1)} %copy-done.9), kind=kOutput, calls=%fused_computation.41 | convolution fusion | flops 916389888 | bytes 5406720 | tf_op jit(solution)/shard_map/dot_general | solution.py:8
  174.3 14.9 %all-to-all-done.2 = bf16[8,72,1024]{2,1,0:T(8,128)(2,1)S(1)} async-done(((bf16[8,72,1024]{2,1,0:T(8,128)(2,1)}), bf16[8,72,1024]{2,1,0:T(8,128)(2,1)S(1)}, u32[]{:S(2)}, u32[]{:S(2)}) %all-to-all-start.2) | async-done | bytes 1179680 | tf_op jit(solution)/shard_map/all_to_all | solution.py:75
  189.2 2.8 %gather_fusion.3 = bf16[512,1024]{1,0:T(8,128)(2,1)} fusion(bf16[576,1024]{1,0:T(8,128)(2,1)S(1)} %bitcast.45, s32[1024]{0:T(1024)S(1)} %pad_clamp_fusion), kind=kCustom, calls=%fused_computation.3 | custom fusion | bytes 2099200 | tf_op jit(solution)/shard_map/gather | solution.py:87
  191.9 1.5 gather.18
  193.4 2.1 %reduce_sum.25 = bf16[128,1024]{1,0:T(8,128)(2,1)} reduce(bf16[128,4,1024]{2,1,0:T(4,128)(2,1)S(1)} %gather.18, bf16[]{:T(256)} %constant.14.clone.1), dimensions={1}, to_apply=%region_7.8 | reduce | flops 393216 | bytes 1310722 | tf_op jit(solution)/shard_map/reduce_sum | solution.py:88
  (44 shorter events, 3.8 us)
Async XLA Ops:
  7.2 54.0 %copy-start = (bf16[1,1024,768]{2,1,0:T(8,128)(2,1)S(1)}, bf16[1,1024,768]{2,1,0:T(8,128)(2,1)}, u32[]{:S(2)}) copy-start(bf16[1,1024,768]{2,1,0:T(8,128)(2,1)} %param.11) | copy-start | bytes 4718596
  17.6 7.4 %copy-start.2 = (bf16[128,1024]{1,0:T(8,128)(2,1)S(1)}, bf16[128,1024]{1,0:T(8,128)(2,1)}, u32[]{:S(2)}) copy-start(bf16[128,1024]{1,0:T(8,128)(2,1)} %param.8) | copy-start | bytes 786436
  17.6 36.1 %all-to-all-start.1 = ((bf16[8,72,1024]{2,1,0:T(8,128)(2,1)}), bf16[8,72,1024]{2,1,0:T(8,128)(2,1)}, u32[]{:S(2)}, u32[]{:S(2)}) async-start(bf16[8,72,1024]{2,1,0:T(8,128)(2,1)} %bitcast.7), calls=%async_computation.1 | async-start | bytes 2359296 | tf_op jit(solution)/shard_map/all_to_all | solution.py:60
  25.1 2.9 %copy-start.3 = (f32[128,4]{0,1:T(4,128)S(1)}, f32[128,4]{0,1:T(4,128)}, u32[]{:S(2)}) copy-start(f32[128,4]{0,1:T(4,128)} %param.10) | copy-start | bytes 6148
  53.8 32.4 %all-to-all-start = ((bf16[8,72,1024]{2,1,0:T(8,128)(2,1)}), bf16[8,72,1024]{2,1,0:T(8,128)(2,1)S(1)}, u32[]{:S(2)}, u32[]{:S(2)}) async-start(bf16[8,72,1024]{2,1,0:T(8,128)(2,1)} %fusion), calls=%async_computation | async-start | bytes 2359296 | tf_op jit(solution)/shard_map/all_to_all | solution.py:61
  57.4 92.3 %all-reduce.5.cloned.1.call-start = ((), (), s32[]{:S(2)}) async-start(), calls=%async_computation.3 | async-start | bytes 5308416 | tf_op jit(solution)/shard_map/psum | solution.py:70
  86.1 3.9 %copy-start.1 = (bf16[8,72,1024]{2,1,0:T(8,128)(2,1)}, bf16[8,72,1024]{2,1,0:T(8,128)(2,1)S(1)}, u32[]{:S(2)}) copy-start(bf16[8,72,1024]{2,1,0:T(8,128)(2,1)S(1)} %all-to-all-done) | copy-start | bytes 3538948
  149.7 3.3 %copy-start.4 = (bf16[1,1024,768]{2,1,0:T(8,128)(2,1)S(1)}, bf16[1,1024,768]{2,1,0:T(8,128)(2,1)}, u32[]{:S(2)}) copy-start(bf16[1,1024,768]{2,1,0:T(8,128)(2,1)} %param.12) | copy-start | bytes 4718596
  149.7 3.4 %copy-start.6 = (bf16[576,768]{1,0:T(8,128)(2,1)S(1)}, bf16[576,768]{1,0:T(8,128)(2,1)}, u32[]{:S(2)}) copy-start(bf16[576,768]{1,0:T(8,128)(2,1)} %get-tuple-element.5) | copy-start | bytes 2654212
  149.7 3.4 %copy-start.8 = (bf16[576,768]{1,0:T(8,128)(2,1)S(1)}, bf16[576,768]{1,0:T(8,128)(2,1)}, u32[]{:S(2)}) copy-start(bf16[576,768]{1,0:T(8,128)(2,1)} %get-tuple-element.6) | copy-start | bytes 2654212
  155.3 33.8 %all-to-all-start.2 = ((bf16[8,72,1024]{2,1,0:T(8,128)(2,1)}), bf16[8,72,1024]{2,1,0:T(8,128)(2,1)S(1)}, u32[]{:S(2)}, u32[]{:S(2)}) async-start(bf16[8,72,1024]{2,1,0:T(8,128)(2,1)} %bitcast.49), calls=%async_computation.2 | async-start | bytes 2359296 | tf_op jit(solution)/shard_map/all_to_all | solution.py:75
  160.9 4.9 %copy-start.7 = (bf16[576,768]{1,0:T(8,128)(2,1)S(1)}, bf16[576,768]{1,0:T(8,128)(2,1)}, u32[]{:S(2)}) copy-start(bf16[576,768]{1,0:T(8,128)(2,1)} %get-tuple-element.5) | copy-start | bytes 2654212
  160.9 4.9 %copy-start.9 = (bf16[576,768]{1,0:T(8,128)(2,1)S(1)}, bf16[576,768]{1,0:T(8,128)(2,1)}, u32[]{:S(2)}) copy-start(bf16[576,768]{1,0:T(8,128)(2,1)} %get-tuple-element.6) | copy-start | bytes 2654212
  165.7 4.2 %copy-start.5 = (bf16[576,768]{1,0:T(8,128)(2,1)S(1)}, bf16[576,768]{1,0:T(8,128)(2,1)}, u32[]{:S(2)}) copy-start(bf16[576,768]{1,0:T(8,128)(2,1)} %get-tuple-element.4) | copy-start | bytes 2654212
Sparse Core Ops, SparseCore 0:
  90.2 59.5 all-reduce.4
where the time goes:
time: 203 us; the launch traced here: 202 us
  waiting for transfers between devices  118 us (58%)
  matrix products  29.9 us (15%)
  local copies, waits for them, and re-layouts  18.3 us (9%)
  starting transfers between devices  16.6 us (8%)
  between operations  14.2 us (7%)
  other arithmetic  5.5 us (3%)
    psum x1, waiting for transfers between devices, on_device(): lax.psum(up_part.astype(jnp.bfloat16), 'tp').astype(jnp.float32)  59.7 us
    all_to_all x1, waiting for transfers between devices, on_device(): lax.all_to_all(send_dy, 'ep', split_axis=0, concat_axis=0, tiled=True)  21.6 us
    all_to_all x1, waiting for transfers between devices, on_device(): lax.all_to_all(send_x, 'ep', split_axis=0, concat_axis=0, tiled=True)  21.6 us
    all_to_all x1, waiting for transfers between devices, on_device(): lax.all_to_all(dx_rows.reshape(experts, capacity, width_part), 'ep', spli...  14.9 us
    dot_general x3, matrix products, contract_rows(): lax.dot_general(left, right, (((0,), (0,)), ((), ())), preferred_element_...  13.4 us
    dot_general x3, matrix products, contract_cols(): lax.dot_general(left, right, (((1,), (1,)), ((), ())), preferred_element_...  9.42 us
    all_to_all x1, starting transfers between devices, on_device(): lax.all_to_all(send_x, 'ep', split_axis=0, concat_axis=0, tiled=True)  7.44 us
    all_to_all x1, starting transfers between devices, on_device(): lax.all_to_all(dx_rows.reshape(experts, capacity, width_part), 'ep', spli...  5.52 us
  transfers between devices with their start and end apart: 4, of which 4 were waited for; matrix products, arithmetic and copies ran while one was open for 14% of the time, Pallas kernels for 0%

commit v1 on v0

--- a/solution.py
+++ b/solution.py
@@ -67,7 +67,7 @@
     dact_part = contract_cols(recv_dy, down_mat)
     gate, up, dact = (
         lax.psum(gate_part.astype(jnp.bfloat16), "tp").astype(jnp.float32),
-        lax.psum(up_part.astype(jnp.bfloat16), "tp").astype(jnp.float32),
+        jnp.sum(lax.all_gather(up_part.astype(jnp.bfloat16), "tp"), axis=0).astype(jnp.float32),
         lax.psum(dact_part.astype(jnp.bfloat16), "tp").astype(jnp.float32),
     )
     act, dgate, dup = swiglu_back(gate, up, dact)

time: 203 us -> 197 us (0.970)
  blocking collectives: 0 us -> 36.1 us
  waiting for transfers between devices: 118 us -> 83.8 us
  starting transfers between devices: 16.6 us -> 9.97 us
  matrix products: 29.9 us -> 25.2 us
  other arithmetic: 5.5 us -> 8.52 us
    all_to_all x0 -> x1, blocking collectives: none -> 36.1 us  [on_device(): lax.all_to_all(send_x, 'ep', split_axis=0, concat_axis=0, tiled=True)]
    all_to_all x1 -> x0, waiting for transfers between devices: 21.6 us -> none  [on_device(): lax.all_to_all(send_x, 'ep', split_axis=0, concat_axis=0, tiled=True)]
    psum x1, waiting for transfers between devices: 59.7 us -> 41.9 us  [on_device(): lax.psum(dact_part.astype(jnp.bfloat16), 'tp').astype(jnp.float32)]
    all_to_all x1 -> x0, starting transfers between devices: 7.44 us -> none  [on_device(): lax.all_to_all(send_x, 'ep', split_axis=0, concat_axis=0, tiled=True)]
    all_to_all x1, waiting for transfers between devices: 21.6 us -> 25.7 us  [on_device(): lax.all_to_all(send_dy, 'ep', split_axis=0, concat_axis=0, tiled=True)]
    reduce_sum x0 -> x1, other arithmetic: none -> 3.03 us  [on_device(): jnp.sum(lax.all_gather(up_part.astype(jnp.bfloat16), 'tp'), axis=0)]
  transfers between devices with their start and end apart: 4 -> 4, of which waited for: 4 -> 3; matrix products, arithmetic and copies ran while one was open for 14% -> 14% of each run, Pallas kernels for 0% -> 0%
where the time goes in v1:
time: 197 us
  waiting for transfers between devices  83.8 us (43%)
  blocking collectives  36.1 us (18%)
  matrix products  25.2 us (13%)
  local copies, waits for them, and re-layouts  18.8 us (10%)
  between operations  14.3 us (7%)
  starting transfers between devices  9.97 us (5%)
  other arithmetic  8.52 us (4%)
    psum x1, waiting for transfers between devices, on_device(): lax.psum(dact_part.astype(jnp.bfloat16), 'tp').astype(jnp.float32)  41.9 us
    all_to_all x1, blocking collectives, on_device(): lax.all_to_all(send_x, 'ep', split_axis=0, concat_axis=0, tiled=True)  36.1 us
    all_to_all x1, waiting for transfers between devices, on_device(): lax.all_to_all(send_dy, 'ep', split_axis=0, concat_axis=0, tiled=True)  25.7 us
    all_to_all x1, waiting for transfers between devices, on_device(): lax.all_to_all(dx_rows.reshape(experts, capacity, width_part), 'ep', spli...  16.2 us
    dot_general x3, matrix products, contract_rows(): lax.dot_general(left, right, (((0,), (0,)), ((), ())), preferred_element_...  12.1 us
    dot_general x3, matrix products, contract_cols(): lax.dot_general(left, right, (((1,), (1,)), ((), ())), preferred_element_...  9.07 us
    all_to_all x1, starting transfers between devices, on_device(): lax.all_to_all(dx_rows.reshape(experts, capacity, width_part), 'ep', spli...  5.52 us
    all_to_all x1, starting transfers between devices, on_device(): lax.all_to_all(send_dy, 'ep', split_axis=0, concat_axis=0, tiled=True)  4.37 us
  transfers between devices with their start and end apart: 4, of which 3 were waited for; matrix products, arithmetic and copies ran while one was open for 14% of the time, Pallas kernels for 0%

profile of v1, /device:TPU:0, one launch (start us, length us, event | category | flops | bytes accessed | tf_op | source)
XLA Modules:
  0.0 196.8 jit_solution(5963182050243549084)
XLA Ops:
  9.3 1.1 reduce-window.6
  10.8 2.4 %scatter_custom_fusion = s32[576]{0:T(1024)S(1)} fusion(s32[512]{0:T(512)S(1)} %bitcast.55, s32[512]{0:T(512)S(1)} %iota.11, s32[]{:T(128)} %constant.15.clone.1), kind=kCustom, calls=%fused_computation.68 | custom fusion | bytes 2308 | tf_op jit(solution)/shard_map/scatter | solution.py:45
  14.2 2.9 %gather_fusion.2 = bf16[576,1024]{1,0:T(8,128)(2,1)S(1)} fusion(bf16[129,1024]{1,0:T(8,128)(2,1)S(1)} %concatenate.11, s32[1024]{0:T(1024)S(1)} %get-tuple-element.9), kind=kCustom, calls=%fused_computation.2 | custom fusion | bytes 2361600 | tf_op jit(solution)/shard_map/gather | solution.py:51
  17.1 36.1 %all_to_all.15 = bf16[8,72,1024]{2,1,0:T(8,128)(2,1)S(1)} all-to-all(bf16[8,72,1024]{2,1,0:T(8,128)(2,1)S(1)} %bitcast.48), channel_id=1, replica_groups=mesh['ep'=8,'tp'=4] {'ep'}, dimensions={0} | all-to-all | bytes 2359296 | tf_op jit(solution)/shard_map/all_to_all | solution.py:60
  54.3 2.0 %fusion.26 = bf16[576,768]{1,0:T(8,128)(2,1)} fusion(bf16[576,1024]{1,0:T(8,128)(2,1)S(1)} %bitcast.50, bf16[1,1024,768]{2,1,0:T(8,128)(2,1)S(1)} %copy-done.8), kind=kOutput, calls=%fused_computation.45 | convolution fusion | flops 906412032 | bytes 3637248 | tf_op jit(solution)/shard_map/dot_general | solution.py:66
  56.4 2.9 %gather_fusion = bf16[576,1024]{1,0:T(8,128)(2,1)S(1)} fusion(bf16[129,1024]{1,0:T(8,128)(2,1)S(1)} %concatenate.9, s32[1024]{0:T(1024)S(1)} %get-tuple-element.9), kind=kCustom, calls=%fused_computation | custom fusion | bytes 2361600 | tf_op jit(solution)/shard_map/gather | solution.py:52
  59.5 2.6 %gather_fusion.1 = f32[576]{0:T(1024)S(1)} fusion(f32[513]{0:T(1024)S(1)} %pad_maximum_fusion, s32[1024]{0:T(1024)S(1)} %get-tuple-element.8), kind=kCustom, calls=%fused_computation.1 | custom fusion | bytes 6912 | tf_op jit(solution)/shard_map/gather | solution.py:52
  62.1 1.3 fusion
  63.4 4.4 %all-to-all-start = ((bf16[8,72,1024]{2,1,0:T(8,128)(2,1)}), bf16[8,72,1024]{2,1,0:T(8,128)(2,1)}, u32[]{:S(2)}, u32[]{:S(2)}) async-start(bf16[8,72,1024]{2,1,0:T(8,128)(2,1)} %fusion), calls=%async_computation | async-start | bytes 2359296 | tf_op jit(solution)/shard_map/all_to_all | solution.py:61
  67.9 2.0 %fusion.29 = bf16[576,768]{1,0:T(8,128)(2,1)} fusion(bf16[576,1024]{1,0:T(8,128)(2,1)S(1)} %bitcast.52, bf16[1,1024,768]{2,1,0:T(8,128)(2,1)S(1)} %copy-done), kind=kOutput, calls=%fused_computation.46 | convolution fusion | flops 906412032 | bytes 3637248 | tf_op jit(solution)/shard_map/dot_general | solution.py:65
  69.9 25.7 %all-to-all-done = bf16[8,72,1024]{2,1,0:T(8,128)(2,1)} async-done(((bf16[8,72,1024]{2,1,0:T(8,128)(2,1)}), bf16[8,72,1024]{2,1,0:T(8,128)(2,1)}, u32[]{:S(2)}, u32[]{:S(2)}) %all-to-all-start) | async-done | bytes 1179680 | tf_op jit(solution)/shard_map/all_to_all | solution.py:61
  95.5 3.8 %fusion.23 = bf16[576,768]{1,0:T(8,128)(2,1)} fusion(bf16[576,1024]{1,0:T(8,128)(2,1)} %bitcast.5, bf16[1,768,1024]{2,1,0:T(8,128)(2,1)} %param.13), kind=kOutput, calls=%fused_computation.44 | convolution fusion | flops 906412032 | bytes 3637248 | tf_op jit(solution)/shard_map/dot_general | solution.py:14
  99.4 3.0 %reduce_sum.37 = bf16[576,768]{1,0:T(8,128)(2,1)S(1)} reduce(bf16[4,576,768]{2,1,0:T(8,128)(2,1)} %bitcast.49, bf16[]{:T(256)} %constant.14.clone.1), dimensions={0}, to_apply=%region_5.6 | reduce | flops 1327104 | bytes 4423682 | tf_op jit(solution)/shard_map/reduce_sum | solution.py:70
  102.5 41.9 %all-reduce.5.cloned.1.call-done = (bf16[576,768]{1,0:T(8,128)(2,1)}, bf16[576,768]{1,0:T(8,128)(2,1)}) async-done(((bf16[576,768]{1,0:T(8,128)(2,1)}, bf16[576,768]{1,0:T(8,128)(2,1)}), (bf16[576,768]{1,0:T(8,128)(2,1)}, bf16[576,768]{1,0:T(8,128)(2,1)})) %all-reduce.5.cloned.1.call-update) | async-done | bytes 1769488 | tf_op jit(solution)/shard_map/psum | solution.py:71
  144.4 3.1 %fusion.11 = f32[576,1024]{1,0:T(8,128)S(1)} fusion(bf16[1,1024,768]{2,1,0:T(8,128)(2,1)S(1)} %copy-done, bf16[576,768]{1,0:T(8,128)(2,1)S(1)} %reduce_sum.37, bf16[576,768]{1,0:T(8,128)(2,1)} %get-tuple-element.4, bf16[576,768]{1,0:T(8,128)(2,1)} %get-tuple-element.5), kind=kOutput, calls=%fused_computation.32 | convolution fusion | flops 911720448 | bytes 6586368 | tf_op jit(solution)/shard_map/dot_general | solution.py:14
  147.5 2.2 %add_convert_fusion = bf16[576,1024]{1,0:T(8,128)(2,1)} fusion(f32[576,1024]{1,0:T(8,128)S(1)} %fusion.11, bf16[1,1024,768]{2,1,0:T(8,128)(2,1)S(1)} %copy-done.9, bf16[576,768]{1,0:T(8,128)(2,1)S(1)} %copy-done.12, bf16[576,768]{1,0:T(8,128)(2,1)S(1)} %copy-done.10), kind=kOutput, calls=%fused_computation.16 | convolution fusion | flops 910688256 | bytes 6881280 | tf_op jit(solution)/shard_map/dot_general | solution.py:14
  149.7 5.5 %all-to-all-start.2 = ((bf16[8,72,1024]{2,1,0:T(8,128)(2,1)}), bf16[8,72,1024]{2,1,0:T(8,128)(2,1)S(1)}, u32[]{:S(2)}, u32[]{:S(2)}) async-start(bf16[8,72,1024]{2,1,0:T(8,128)(2,1)} %bitcast.54), calls=%async_computation.2 | async-start | bytes 2359296 | tf_op jit(solution)/shard_map/all_to_all | solution.py:75
  155.2 4.7 %fusion.21 = bf16[1,1024,768]{2,1,0:T(8,128)(2,1)} fusion(bf16[576,1024]{1,0:T(8,128)(2,1)} %bitcast.51, bf16[576,768]{1,0:T(8,128)(2,1)} %get-tuple-element.5, bf16[576,768]{1,0:T(8,128)(2,1)} %get-tuple-element.4), kind=kOutput, calls=%fused_computation.42 | convolution fusion | flops 914178048 | bytes 4521984 | tf_op jit(solution)/shard_map/dot_general | solution.py:8
  160.0 4.3 %fusion.22 = bf16[1,768,1024]{2,1,0:T(8,128)(2,1)} fusion(bf16[576,1024]{1,0:T(8,128)(2,1)} %bitcast.5, bf16[576,768]{1,0:T(8,128)(2,1)S(1)} %copy-done.5, bf16[576,768]{1,0:T(8,128)(2,1)S(1)} %copy-done.13), kind=kOutput, calls=%fused_computation.43 | convolution fusion | flops 914178048 | bytes 4521984 | tf_op jit(solution)/shard_map/dot_general | solution.py:8
  164.3 3.1 %fusion.20 = bf16[1,1024,768]{2,1,0:T(8,128)(2,1)} fusion(bf16[576,1024]{1,0:T(8,128)(2,1)S(1)} %bitcast.53, bf16[576,768]{1,0:T(8,128)(2,1)S(1)} %copy-done.5, bf16[576,768]{1,0:T(8,128)(2,1)S(1)} %copy-done.11, bf16[576,768]{1,0:T(8,128)(2,1)S(1)} %copy-done.13), kind=kOutput, calls=%fused_computation.41 | convolution fusion | flops 916389888 | bytes 5406720 | tf_op jit(solution)/shard_map/dot_general | solution.py:8
  167.4 16.2 %all-to-all-done.2 = bf16[8,72,1024]{2,1,0:T(8,128)(2,1)S(1)} async-done(((bf16[8,72,1024]{2,1,0:T(8,128)(2,1)}), bf16[8,72,1024]{2,1,0:T(8,128)(2,1)S(1)}, u32[]{:S(2)}, u32[]{:S(2)}) %all-to-all-start.2) | async-done | bytes 1179680 | tf_op jit(solution)/shard_map/all_to_all | solution.py:75
  183.6 2.8 %gather_fusion.3 = bf16[512,1024]{1,0:T(8,128)(2,1)} fusion(bf16[576,1024]{1,0:T(8,128)(2,1)S(1)} %bitcast.46, s32[1024]{0:T(1024)S(1)} %pad_clamp_fusion), kind=kCustom, calls=%fused_computation.3 | custom fusion | bytes 2099200 | tf_op jit(solution)/shard_map/gather | solution.py:87
  186.4 1.5 gather.18
  187.8 2.1 %reduce_sum.38 = bf16[128,1024]{1,0:T(8,128)(2,1)} reduce(bf16[128,4,1024]{2,1,0:T(4,128)(2,1)S(1)} %gather.18, bf16[]{:T(256)} %constant.14.clone.1), dimensions={1}, to_apply=%region_7.8 | reduce | flops 393216 | bytes 1310722 | tf_op jit(solution)/shard_map/reduce_sum | solution.py:88
  (55 shorter events, 4.9 us)
Async XLA Ops:
  7.2 60.7 %copy-start = (bf16[1,1024,768]{2,1,0:T(8,128)(2,1)S(1)}, bf16[1,1024,768]{2,1,0:T(8,128)(2,1)}, u32[]{:S(2)}) copy-start(bf16[1,1024,768]{2,1,0:T(8,128)(2,1)} %param.11) | copy-start | bytes 4718596
  7.2 92.2 %all-gather.3.cloned.1.call-start = ((), (), s32[]{:S(2)}) async-start(), calls=%async_computation.3 | async-start | bytes 4423680 | tf_op jit(solution)/shard_map/all_gather | solution.py:70
  17.1 37.2 %copy-start.8 = (bf16[1,1024,768]{2,1,0:T(8,128)(2,1)S(1)}, bf16[1,1024,768]{2,1,0:T(8,128)(2,1)}, u32[]{:S(2)}) copy-start(bf16[1,1024,768]{2,1,0:T(8,128)(2,1)} %param.12) | copy-start | bytes 4718596
  53.3 1.0 copy-start.1
  54.3 2.0 %copy-start.6 = (bf16[128,1024]{1,0:T(8,128)(2,1)S(1)}, bf16[128,1024]{1,0:T(8,128)(2,1)}, u32[]{:S(2)}) copy-start(bf16[128,1024]{1,0:T(8,128)(2,1)} %param.8) | copy-start | bytes 786436
  56.3 2.9 %copy-start.7 = (f32[128,4]{0,1:T(4,128)S(1)}, f32[128,4]{0,1:T(4,128)}, u32[]{:S(2)}) copy-start(f32[128,4]{0,1:T(4,128)} %param.10) | copy-start | bytes 6148
  63.4 4.4 %copy-start.2 = (bf16[8,72,1024]{2,1,0:T(8,128)(2,1)S(1)}, bf16[8,72,1024]{2,1,0:T(8,128)(2,1)}, u32[]{:S(2)}) copy-start(bf16[8,72,1024]{2,1,0:T(8,128)(2,1)} %copy-done.1) | copy-start | bytes 3538948
  63.4 32.1 %all-to-all-start = ((bf16[8,72,1024]{2,1,0:T(8,128)(2,1)}), bf16[8,72,1024]{2,1,0:T(8,128)(2,1)}, u32[]{:S(2)}, u32[]{:S(2)}) async-start(bf16[8,72,1024]{2,1,0:T(8,128)(2,1)} %fusion), calls=%async_computation | async-start | bytes 2359296 | tf_op jit(solution)/shard_map/all_to_all | solution.py:61
  67.8 76.6 %all-reduce.5.cloned.1.call-start = ((), (), s32[]{:S(2)}) async-start(), calls=%async_computation.4 | async-start | bytes 3538944 | tf_op jit(solution)/shard_map/psum | solution.py:71
  102.4 45.0 %copy-start.4 = (bf16[576,768]{1,0:T(8,128)(2,1)}, bf16[576,768]{1,0:T(8,128)(2,1)S(1)}, u32[]{:S(2)}) copy-start(bf16[576,768]{1,0:T(8,128)(2,1)S(1)} %reduce_sum.37) | copy-start | bytes 2654212
  144.4 3.1 %copy-start.9 = (bf16[1,1024,768]{2,1,0:T(8,128)(2,1)S(1)}, bf16[1,1024,768]{2,1,0:T(8,128)(2,1)}, u32[]{:S(2)}) copy-start(bf16[1,1024,768]{2,1,0:T(8,128)(2,1)} %param.12) | copy-start | bytes 4718596
  144.4 3.1 %copy-start.10 = (bf16[576,768]{1,0:T(8,128)(2,1)S(1)}, bf16[576,768]{1,0:T(8,128)(2,1)}, u32[]{:S(2)}) copy-start(bf16[576,768]{1,0:T(8,128)(2,1)} %get-tuple-element.4) | copy-start | bytes 2654212
  144.4 3.1 %copy-start.12 = (bf16[576,768]{1,0:T(8,128)(2,1)S(1)}, bf16[576,768]{1,0:T(8,128)(2,1)}, u32[]{:S(2)}) copy-start(bf16[576,768]{1,0:T(8,128)(2,1)} %get-tuple-element.5) | copy-start | bytes 2654212
  149.7 33.9 %all-to-all-start.2 = ((bf16[8,72,1024]{2,1,0:T(8,128)(2,1)}), bf16[8,72,1024]{2,1,0:T(8,128)(2,1)S(1)}, u32[]{:S(2)}, u32[]{:S(2)}) async-start(bf16[8,72,1024]{2,1,0:T(8,128)(2,1)} %bitcast.54), calls=%async_computation.2 | async-start | bytes 2359296 | tf_op jit(solution)/shard_map/all_to_all | solution.py:75
  155.2 4.7 %copy-start.5 = (bf16[576,768]{1,0:T(8,128)(2,1)S(1)}, bf16[576,768]{1,0:T(8,128)(2,1)}, u32[]{:S(2)}) copy-start(bf16[576,768]{1,0:T(8,128)(2,1)} %copy-done.4) | copy-start | bytes 2654212
  155.2 4.7 %copy-start.13 = (bf16[576,768]{1,0:T(8,128)(2,1)S(1)}, bf16[576,768]{1,0:T(8,128)(2,1)}, u32[]{:S(2)}) copy-start(bf16[576,768]{1,0:T(8,128)(2,1)} %get-tuple-element.5) | copy-start | bytes 2654212
  160.0 4.4 %copy-start.3 = (bf16[8,72,1024]{2,1,0:T(8,128)(2,1)S(1)}, bf16[8,72,1024]{2,1,0:T(8,128)(2,1)}, u32[]{:S(2)}) copy-start(bf16[8,72,1024]{2,1,0:T(8,128)(2,1)} %copy-done.1) | copy-start | bytes 3538948
  160.0 4.4 %copy-start.11 = (bf16[576,768]{1,0:T(8,128)(2,1)S(1)}, bf16[576,768]{1,0:T(8,128)(2,1)}, u32[]{:S(2)}) copy-start(bf16[576,768]{1,0:T(8,128)(2,1)} %get-tuple-element.4) | copy-start | bytes 2654212
Sparse Core Ops, SparseCore 0:
  56.4 29.4 all-gather.2
  99.5 44.8 all-reduce.4
